TPU v7x, 256 devices: a whole 4x4x8 slice. The times are simulated.
256 devices in a mesh: col: 4 (over z_lo, core), dp: 64 (over y, x, z_hi).
Axes of the slice: x: 4, y: 4, z: 8 (z_hi: 4, z_lo: 2; z = z_hi * 2 + z_lo), core: 2. Of those that a mesh axis runs over, the one named last changes fastest.
Arguments:
- layer_input: bfloat16 [8192, 8192], P('dp', 'col'), may hold values from -6 to 6
- query_cotangent: bfloat16 [8192, 4096], P('dp'), may hold values from -0.06591797 to 0.06591797
- key_cotangent: bfloat16 [8192, 1024], P('dp'), may hold values from -0.06591797 to 0.06591797
- up_cotangent: bfloat16 [8192, 14336], P('dp'), may hold values from -0.06591797 to 0.06591797
- query_weight: bfloat16 [4096, 8192], P('dp', 'col'), may hold values from -24 to 24
- key_weight: bfloat16 [1024, 8192], P('dp', 'col'), may hold values from -24 to 24
- up_weight: bfloat16 [14336, 8192], P('dp', 'col'), may hold values from -24 to 24
- moment_query: bfloat16 [4096, 8192], P('dp', 'col'), may hold values from -3 to 3
- moment_key: bfloat16 [1024, 8192], P('dp', 'col'), may hold values from -3 to 3
- moment_up: bfloat16 [14336, 8192], P('dp', 'col'), may hold values from -3 to 3
- second_query: bfloat16 [4096, 8192], P('dp', 'col'), may hold values from 0.25 to 4
- second_key: bfloat16 [1024, 8192], P('dp', 'col'), may hold values from 0.25 to 4
- second_up: bfloat16 [14336, 8192], P('dp', 'col'), may hold values from 0.25 to 4
Outputs:
- updated_query: bfloat16 [4096, 8192], P('dp', 'col')
- updated_key: bfloat16 [1024, 8192], P('dp', 'col')
- updated_up: bfloat16 [14336, 8192], P('dp', 'col')
- mean_query: bfloat16 [4096, 8192], P('dp', 'col')
- mean_key: bfloat16 [1024, 8192], P('dp', 'col')
- mean_up: bfloat16 [14336, 8192], P('dp', 'col')
- square_query: bfloat16 [4096, 8192], P('dp', 'col')
- square_key: bfloat16 [1024, 8192], P('dp', 'col')
- square_up: bfloat16 [14336, 8192], P('dp', 'col')
All inputs are finite; a program needn't handle non-finite values.
Results may differ from a plain program's by a relative error of at most 0.001.
Values may be sent and summed in bfloat16 or wider, within the bound.
A program may use at most 128 MiB of HBM per device.

v0:
```python
import jax
import jax.numpy as jnp
from jax import lax
from jax.sharding import PartitionSpec as P

beta_one = 0.9
beta_two = 0.95
rate = 0.1
eps_adam = 1e-08
eps_norm = 1e-06


def contract_tokens(cotangent_rows, inputs):
    return lax.dot_general(
        cotangent_rows, inputs, (((0,), (0,)), ((), ())), preferred_element_type=jnp.float32
    )


def optimizer_pass(gradient, weight, moment, second):
    first = beta_one * moment.astype(jnp.float32) + (1.0 - beta_one) * gradient
    square = beta_two * second.astype(jnp.float32) + (1.0 - beta_two) * gradient * gradient
    step = weight.astype(jnp.float32) - rate * first / (jnp.sqrt(square) + eps_adam)
    partial_power = jnp.sum(step * step, axis=1)
    return (step, first.astype(jnp.bfloat16), square.astype(jnp.bfloat16), partial_power)


def finish_rows(step, total_power, width):
    scale = jnp.sqrt(total_power / width + eps_norm)
    return (step / scale[:, None]).astype(jnp.bfloat16)


def per_device(
    layer_input,
    query_cotangent,
    key_cotangent,
    up_cotangent,
    query_weight,
    key_weight,
    up_weight,
    moment_query,
    moment_key,
    moment_up,
    second_query,
    second_key,
    second_up,
):
    groups = lax.axis_size("dp")
    tok_local = layer_input.shape[0]
    query_rows = query_weight.shape[0]
    key_rows = key_weight.shape[0]
    up_rows = up_weight.shape[0]
    all_rows = query_rows + key_rows + up_rows
    width = layer_input.shape[1] * lax.axis_size("col")
    joined = jnp.concatenate(
        [
            query_cotangent.reshape(tok_local, groups, query_rows),
            key_cotangent.reshape(tok_local, groups, key_rows),
            up_cotangent.reshape(tok_local, groups, up_rows),
        ],
        axis=2,
    )
    owned = lax.all_to_all(joined, "dp", split_axis=1, concat_axis=0, tiled=True).reshape(
        -1, all_rows
    )
    gathered = lax.all_gather(layer_input, "dp", axis=0, tiled=True)
    gradient = contract_tokens(owned, gathered)
    grad_query = gradient[:query_rows]
    grad_key = gradient[query_rows : query_rows + key_rows]
    grad_up = gradient[query_rows + key_rows :]
    step_query, first_query, sq_query, power_query = optimizer_pass(
        grad_query, query_weight, moment_query, second_query
    )
    step_key, first_key, sq_key, power_key = optimizer_pass(
        grad_key, key_weight, moment_key, second_key
    )
    step_up, first_up, sq_up, power_up = optimizer_pass(grad_up, up_weight, moment_up, second_up)
    total_query, total_key, total_up = lax.psum((power_query, power_key, power_up), "col")
    new_query = finish_rows(step_query, total_query, width)
    new_key = finish_rows(step_key, total_key, width)
    new_up = finish_rows(step_up, total_up, width)
    return (new_query, new_key, new_up, first_query, first_key, first_up, sq_query, sq_key, sq_up)


def solution(mesh):
    placed = (
        P("dp", "col"),
        P("dp", None),
        P("dp", None),
        P("dp", None),
        P("dp", "col"),
        P("dp", "col"),
        P("dp", "col"),
        P("dp", "col"),
        P("dp", "col"),
        P("dp", "col"),
        P("dp", "col"),
        P("dp", "col"),
        P("dp", "col"),
    )
    return jax.shard_map(
        per_device,
        mesh=mesh,
        in_specs=placed,
        out_specs=(
            P("dp", "col"),
            P("dp", "col"),
            P("dp", "col"),
            P("dp", "col"),
            P("dp", "col"),
            P("dp", "col"),
            P("dp", "col"),
            P("dp", "col"),
            P("dp", "col"),
        ),
        check_vma=False,
    )
```

profile of v0, /device:TPU:1, one launch (start us, length us, event | category | flops | bytes accessed | tf_op | source)
XLA Modules:
  0.0 439.6 jit_solution(7235209890121948709)
XLA Ops:
  7.2 0.0 all-gather.2.cloned.1.call-start
  7.2 0.7 all-gather.2.cloned.1.call-update
  7.9 0.0 copy-start
  7.9 0.0 copy-start.6
  7.9 6.1 %copy.24 = bf16[128,14336]{0,1:T(8,128)(2,1)} copy(bf16[128,14336]{1,0:T(8,128)(2,1)} %param.16) | data formatting | bytes 7340032 | tf_op args[3]
  14.1 0.0 copy-done
  14.1 0.7 copy.22
  14.7 0.0 copy-done.6
  14.7 0.2 copy.23
  14.9 2.2 pad_maximum_fusion
  17.2 185.8 %all_to_all.15 = bf16[128,64,304]{0,2,1:T(8,128)(2,1)S(1)} all-to-all(bf16[128,64,304]{0,2,1:T(8,128)(2,1)S(1)} %pad_maximum_fusion), channel_id=1, replica_groups=mesh['col'=4,'dp'=64] {'dp'}, dimensions={1} | all-to-all | bytes 9961472 | tf_op jit(solution)/shard_map/all_to_all | solution.py:62
  203.0 3.6 copy.25
  206.7 183.5 %all-gather.2.cloned.1.call-done = bf16[8192,2048]{1,0:T(8,128)(2,1)} async-done(((bf16[128,2048]{1,0:T(8,128)(2,1)}), bf16[8192,2048]{1,0:T(8,128)(2,1)}) %all-gather.2.cloned.1.call-update) | async-done | bytes 33554448 | tf_op jit(solution)/shard_map/all_gather | solution.py:65
  390.2 26.3 %fusion = f32[304,2048]{1,0:T(8,128)S(1)} fusion(bf16[8192,2048]{1,0:T(8,128)(2,1)} %all-gather.2.cloned.1.call-done, bf16[38,8,64,128]{3,2,1,0:T(8,128)(2,1)} %bitcast.16), kind=kOutput, calls=%fused_computation | convolution fusion | flops 10200547328 | bytes 41025536 | tf_op jit(solution)/shard_map/dot_general | solution.py:14
  416.5 0.0 copy-done.1
  416.5 0.0 copy-done.2
  416.5 0.0 copy-start.3
  416.5 0.0 copy-start.4
  416.5 0.0 copy-start.5
  416.5 0.0 copy-start.7
  416.5 0.0 copy-start.8
  416.6 0.0 copy-start.9
  416.6 4.2 multiply_reduce_fusion
  420.7 0.0 copy-done.3
  420.7 0.0 copy-done.4
  420.8 0.0 copy-done.5
  420.8 1.3 multiply_reduce_fusion.1
  422.1 0.9 multiply_reduce_fusion.2
  423.0 7.1 %all-reduce = (f32[64]{0:T(128)S(1)}, f32[16]{0:T(128)S(1)}, f32[224]{0:T(256)S(1)}) all-reduce(f32[64]{0:T(128)S(1)} %get-tuple-element.16, f32[16]{0:T(128)S(1)} %get-tuple-element.14, f32[224]{0:T(256)S(1)} %get-tuple-element.12), channel_id=1, replica_groups=mesh['col'=4,'dp'=64] {'col'}, use_global_device_ids=true, to_apply=%region_1.0 | all-reduce | flops 304 | bytes 2432 | tf_op jit(solution)/shard_map/psum | solution.py:77
  430.1 1.1 divide_convert_fusion
  431.2 0.7 divide_convert_fusion.2
  431.9 0.8 divide_convert_fusion.1
  (8 shorter events, 0.0 us)
Async XLA Ops:
  7.2 383.0 %all-gather.2.cloned.1.call-start = ((), (), s32[]{:S(2)}) async-start(), calls=%async_computation.1 | async-start | bytes 34078720 | tf_op jit(solution)/shard_map/all_gather | solution.py:65
  7.9 6.2 %copy-start = (bf16[128,4096]{1,0:T(8,128)(2,1)S(1)}, bf16[128,4096]{1,0:T(8,128)(2,1)}, u32[]{:S(2)}) copy-start(bf16[128,4096]{1,0:T(8,128)(2,1)} %param.14) | copy-start | bytes 3145732
  7.9 6.8 %copy-start.6 = (bf16[128,1024]{1,0:T(8,128)(2,1)S(1)}, bf16[128,1024]{1,0:T(8,128)(2,1)}, u32[]{:S(2)}) copy-start(bf16[128,1024]{1,0:T(8,128)(2,1)} %param.15) | copy-start | bytes 786436
  390.2 26.3 %copy-start.1 = (bf16[224,2048]{1,0:T(8,128)(2,1)S(1)}, bf16[224,2048]{1,0:T(8,128)(2,1)}, u32[]{:S(2)}) copy-start(bf16[224,2048]{1,0:T(8,128)(2,1)} %param.25) | copy-start | bytes 2752516
  390.2 26.3 %copy-start.2 = (bf16[224,2048]{1,0:T(8,128)(2,1)S(1)}, bf16[224,2048]{1,0:T(8,128)(2,1)}, u32[]{:S(2)}) copy-start(bf16[224,2048]{1,0:T(8,128)(2,1)} %param.22) | copy-start | bytes 2752516
  416.5 4.2 copy-start.3
  416.5 4.2 copy-start.4
  416.5 4.2 copy-start.5
  416.5 5.5 %copy-start.7 = (bf16[16,2048]{1,0:T(8,128)(2,1)S(1)}, bf16[16,2048]{1,0:T(8,128)(2,1)}, u32[]{:S(2)}) copy-start(bf16[16,2048]{1,0:T(8,128)(2,1)} %param.24) | copy-start | bytes 196612
  416.5 5.5 %copy-start.8 = (bf16[16,2048]{1,0:T(8,128)(2,1)S(1)}, bf16[16,2048]{1,0:T(8,128)(2,1)}, u32[]{:S(2)}) copy-start(bf16[16,2048]{1,0:T(8,128)(2,1)} %param.21) | copy-start | bytes 196612
  416.6 5.5 %copy-start.9 = (bf16[16,2048]{1,0:T(8,128)(2,1)S(1)}, bf16[16,2048]{1,0:T(8,128)(2,1)}, u32[]{:S(2)}) copy-start(bf16[16,2048]{1,0:T(8,128)(2,1)} %param.18) | copy-start | bytes 196612
Sparse Core Ops, SparseCore 0:
  11.3 378.8 all-gather.1
where the time goes:
time: 440 us
  blocking collectives  193 us (44%)
  waiting for transfers between devices  184 us (42%)
  matrix products  26.3 us (6%)
  between operations  14.2 us (3%)
  other arithmetic  11.3 us (3%)
  local copies, waits for them, and re-layouts  10.7 us (2%)
    all_to_all x1, blocking collectives, per_device(): lax.all_to_all(joined, 'dp', split_axis=1, concat_axis=0, tiled=True)  186 us
    all_gather x1, waiting for transfers between devices, per_device(): gathered = lax.all_gather(layer_input, 'dp', axis=0, tiled=True)  184 us
    dot_general x1, matrix products, contract_tokens(): lax.dot_general(cotangent_rows, inputs, (((0,), (0,)), ((), ())), preferr...  26.3 us
  transfers between devices with their start and end apart: 1, of which 1 were waited for; matrix products, arithmetic and copies ran while one was open for 3% of the time, Pallas kernels for 0%

commit v1 on v0

v1 whole, which is shorter than its diff:
```python
import functools

import jax
import jax.numpy as jnp
from jax import lax
from jax.experimental import pallas as pl
from jax.experimental.pallas import tpu as pltpu
from jax.sharding import PartitionSpec as P

beta_one = 0.9
beta_two = 0.95
rate = 0.1
eps_adam = 1e-08
eps_norm = 1e-06

MESH = pl.DeviceIdType.MESH
CHUNKS = 8
LANES = 128


def place():
    dp = lax.axis_index("dp")
    col = lax.axis_index("col")
    return dp // 16, lax.rem(dp // 4, 4), lax.rem(dp, 4), col // 2, lax.rem(col, 2)


def wrap(v):
    return lax.rem(v + 8, 4)


def exchange_kernel(
    ct_ref, x_ref, g_ref, c_buf, x_buf, p_buf, r_buf, ssem, rsem, lsem
):
    y, x, z, lo, core = place()
    toward = 2 * lo - 1
    rows = g_ref.shape[0]
    half = 2 * rows
    width = x_ref.shape[1] // CHUNKS

    def device(dy=0, dx=0, dz=0, flip_lo=False, flip_core=False):
        lo_to = 1 - lo if flip_lo else lo
        core_to = 1 - core if flip_core else core
        return {
            "dp": wrap(y + dy) * 16 + wrap(x + dx) * 4 + wrap(z + dz),
            "col": lo_to * 2 + core_to,
        }

    peers = [device(dy=d) for d in (1, 2, 3)]
    peers += [device(dz=d) for d in (1, 2, 3)]
    peers += [device(dx=d) for d in (1, 3)]
    peers += [device(dy=d, dz=toward, flip_lo=True) for d in range(4)]
    peers += [device(dy=d, dz=2, flip_lo=True) for d in range(4)]
    peers += [device(flip_lo=True), device(flip_core=True)]
    barrier = pltpu.get_barrier_semaphore()
    for peer in peers:
        pl.semaphore_signal(barrier, inc=1, device_id=peer, device_id_type=MESH)
    pl.semaphore_wait(barrier, len(peers))

    used = [0]
    pending = []

    def remote(src, dst, to):
        k = used[0]
        used[0] += 1
        return pltpu.make_async_remote_copy(
            src_ref=src,
            dst_ref=dst,
            send_sem=ssem.at[k],
            recv_sem=rsem.at[k],
            device_id=to,
            device_id_type=MESH,
        )

    def go(copy):
        copy.start()
        pending.append(copy)
        return copy

    def c_slot(slot):
        lanes = pl.ds(pl.multiple_of(slot * LANES, LANES), LANES)
        return c_buf.at[pl.ds(pl.multiple_of(core * half, 16), half), lanes]

    def ct_piece(dy, dz):
        return ct_ref.at[wrap(y + dy) * 4 + wrap(z + dz)]

    def send_c(slot, dy, dz, flip):
        return go(remote(ct_piece(dy, dz), c_slot(slot), device(dy=dy, dz=dz, flip_lo=flip)))

    def cols(j):
        return pl.ds(j * width, width)

    order = (0, 1, 3, 2)
    side = wrap(-toward)
    facing = [send_c(wrap(-dy) * 4 + side, dy, toward, True) for dy in order]
    far = [send_c(wrap(-(lo + 2 * i)) * 4 + 2, lo + 2 * i, 2, True) for i in range(2)]
    near = [send_c(((-dy) % 4) * 4, dy, 0, False) for dy in (1, 3, 2)]
    own_c = pltpu.make_async_copy(ct_piece(0, 0), c_slot(0), lsem.at[0])
    own_c.start()
    own_x = pltpu.make_async_copy(x_ref, x_buf.at[pl.ds(0, LANES)], lsem.at[1])
    own_x.start()
    own_up = go(remote(x_ref, x_buf.at[pl.ds(12 * LANES, LANES)], device(dy=1)))
    own_down = go(remote(x_ref, x_buf.at[pl.ds(4 * LANES, LANES)], device(dy=3)))
    along_z = []
    for j in range(CHUNKS):
        along_z.append(
            [
                go(
                    remote(
                        x_ref.at[:, cols(j)],
                        x_buf.at[pl.ds(((-dz) % 4) * LANES, LANES), cols(j)],
                        device(dz=dz),
                    )
                )
                for dz in (1, 3, 2)
            ]
        )

    def share(slot):
        place_at = c_slot(slot)
        return go(remote(place_at, place_at, device(flip_core=True)))

    def pass_on(slot):
        place_at = c_slot(slot)
        return go(remote(place_at, place_at, device(flip_lo=True)))

    shared = []
    own_c.wait()
    shared.append(share(0))
    for copy, dy in zip(near, (1, 3, 2)):
        copy.wait_recv()
        shared.append(share(((-dy) % 4) * 4))
    passed = []
    mine = wrap(toward)
    for copy, dy in zip(facing, order):
        copy.wait_recv()
        slot = wrap(-dy) * 4 + mine
        passed.append(pass_on(slot))
        shared.append(share(slot))
    for i, copy in enumerate(far):
        copy.wait_recv()
        slot = wrap(-((1 - lo) + 2 * i)) * 4 + 2
        passed.append(pass_on(slot))
        shared.append(share(slot))
    own_up.wait_recv()
    own_fwd = go(
        remote(
            x_buf.at[pl.ds(12 * LANES, LANES)],
            x_buf.at[pl.ds(8 * LANES, LANES)],
            device(dy=1),
        )
    )

    up, down, fwd_up, fwd_down = {}, {}, {}, {}

    def stage_y(j):
        for copy in along_z[j]:
            copy.wait_recv()
        src = x_buf.at[pl.ds(LANES, 3 * LANES), cols(j)]
        up[j] = go(remote(src, x_buf.at[pl.ds(13 * LANES, 3 * LANES), cols(j)], device(dy=1)))
        down[j] = go(remote(src, x_buf.at[pl.ds(5 * LANES, 3 * LANES), cols(j)], device(dy=3)))

    def stage_forward(j):
        up[j].wait_recv()
        fwd_up[j] = go(
            remote(
                x_buf.at[pl.ds(13 * LANES, LANES), cols(j)],
                x_buf.at[pl.ds(9 * LANES, LANES), cols(j)],
                device(dy=1),
            )
        )
        down[j].wait_recv()
        fwd_down[j] = go(
            remote(
                x_buf.at[pl.ds(6 * LANES, 2 * LANES), cols(j)],
                x_buf.at[pl.ds(10 * LANES, 2 * LANES), cols(j)],
                device(dy=3),
            )
        )

    ring = {}

    def ring_send(j, step):
        for way, sign in ((0, 1), (1, -1)):
            target = wrap(x - sign * (step + 1))
            if step > 0:
                ring[j, step - 1, way].wait_recv()
                p_buf[j, target, way] = p_buf[j, target, way] + r_buf[j, step - 1, way]
            ring[j, step, way] = go(
                remote(p_buf.at[j, target, way], r_buf.at[j, step, way], device(dx=sign))
            )

    def finish(j):
        for way in (0, 1):
            ring[j, 2, way].wait_recv()
            at = pl.ds(j * width + way * (width // 2), width // 2)
            g_ref[:, at] = p_buf[j, x, way] + r_buf[j, 2, way]

    def multiply(j):
        fwd_up[j].wait_recv()
        fwd_down[j].wait_recv()

        def one(d, carry):
            lhs = c_buf[pl.ds(pl.multiple_of(d * rows, 16), rows), :]
            out = jnp.dot(lhs, x_buf[:, cols(j)], preferred_element_type=jnp.float32)
            p_buf[j, d, 0] = out[:, : width // 2]
            p_buf[j, d, 1] = out[:, width // 2 :]
            return carry

        lax.fori_loop(0, 4, one, 0)

    stage_y(0)
    other = wrap(-toward)
    for copy, dy in zip(passed[:4], order):
        copy.wait_recv()
        shared.append(share(wrap(-dy) * 4 + other))
    for i, copy in enumerate(passed[4:]):
        copy.wait_recv()
        shared.append(share(wrap(-(lo + 2 * i)) * 4 + 2))
    stage_y(1)
    stage_forward(0)
    own_x.wait()
    own_down.wait_recv()
    own_fwd.wait_recv()
    for copy in shared:
        copy.wait_recv()

    for j in range(CHUNKS + 3):
        if j + 2 < CHUNKS:
            stage_y(j + 2)
        if j + 1 < CHUNKS:
            stage_forward(j + 1)
        if j < CHUNKS:
            multiply(j)
            ring_send(j, 0)
        if 0 <= j - 1 < CHUNKS:
            ring_send(j - 1, 1)
        if 0 <= j - 2 < CHUNKS:
            ring_send(j - 2, 2)
        if 0 <= j - 3 < CHUNKS:
            finish(j - 3)
    for copy in pending:
        copy.wait_send()


def gradient_of(ct, layer_input, rows):
    tokens, width = layer_input.shape
    chunk = width // CHUNKS
    count = 9 + 6 + 16 + 3 + CHUNKS * (3 + 4 + 6)
    return pl.pallas_call(
        exchange_kernel,
        out_shape=jax.ShapeDtypeStruct((rows, width), jnp.float32),
        in_specs=[pl.BlockSpec(memory_space=pl.ANY)] * 2,
        out_specs=pl.BlockSpec(memory_space=pltpu.VMEM),
        scratch_shapes=[
            pltpu.VMEM((4 * rows, 16 * tokens), jnp.bfloat16),
            pltpu.VMEM((16 * tokens, width), jnp.bfloat16),
            pltpu.VMEM((CHUNKS, 4, 2, rows, chunk // 2), jnp.float32),
            pltpu.VMEM((CHUNKS, 3, 2, rows, chunk // 2), jnp.float32),
            pltpu.SemaphoreType.DMA((count,)),
            pltpu.SemaphoreType.DMA((count,)),
            pltpu.SemaphoreType.DMA((2,)),
        ],
        compiler_params=pltpu.CompilerParams(
            collective_id=0, has_side_effects=True, vmem_limit_bytes=60 << 20
        ),
        name="exchange",
    )(ct, layer_input)


def optimizer_pass(gradient, weight, moment, second):
    first = beta_one * moment.astype(jnp.float32) + (1.0 - beta_one) * gradient
    square = beta_two * second.astype(jnp.float32) + (1.0 - beta_two) * gradient * gradient
    step = weight.astype(jnp.float32) - rate * first / (jnp.sqrt(square) + eps_adam)
    partial_power = jnp.sum(step * step, axis=1)
    return (step, first.astype(jnp.bfloat16), square.astype(jnp.bfloat16), partial_power)


def finish_rows(step, total_power, width):
    scale = jnp.sqrt(total_power / width + eps_norm)
    return (step / scale[:, None]).astype(jnp.bfloat16)


def per_device(
    layer_input,
    query_cotangent,
    key_cotangent,
    up_cotangent,
    query_weight,
    key_weight,
    up_weight,
    moment_query,
    moment_key,
    moment_up,
    second_query,
    second_key,
    second_up,
):
    tokens = layer_input.shape[0]
    query_rows = query_weight.shape[0]
    key_rows = key_weight.shape[0]
    up_rows = up_weight.shape[0]
    all_rows = query_rows + key_rows + up_rows
    width = layer_input.shape[1] * lax.axis_size("col")
    core = lax.rem(lax.axis_index("col"), 2)

    def halved(cotangent, rows):
        parts = cotangent.reshape(tokens, 4, 2, 2, 4, rows)
        return lax.dynamic_index_in_dim(parts, core, axis=2, keepdims=False)

    joined = jnp.concatenate(
        [
            halved(query_cotangent, query_rows),
            halved(key_cotangent, key_rows),
            halved(up_cotangent, up_rows),
        ],
        axis=4,
    )
    ct = joined.transpose(1, 3, 2, 4, 0).reshape(16, 2 * all_rows, tokens)
    gradient = gradient_of(ct, layer_input, all_rows)
    grad_query = gradient[:query_rows]
    grad_key = gradient[query_rows : query_rows + key_rows]
    grad_up = gradient[query_rows + key_rows :]
    step_query, first_query, sq_query, power_query = optimizer_pass(
        grad_query, query_weight, moment_query, second_query
    )
    step_key, first_key, sq_key, power_key = optimizer_pass(
        grad_key, key_weight, moment_key, second_key
    )
    step_up, first_up, sq_up, power_up = optimizer_pass(grad_up, up_weight, moment_up, second_up)
    total_query, total_key, total_up = lax.psum((power_query, power_key, power_up), "col")
    new_query = finish_rows(step_query, total_query, width)
    new_key = finish_rows(step_key, total_key, width)
    new_up = finish_rows(step_up, total_up, width)
    return (new_query, new_key, new_up, first_query, first_key, first_up, sq_query, sq_key, sq_up)


def solution(mesh):
    spread = P("dp", "col")
    return jax.shard_map(
        per_device,
        mesh=mesh,
        in_specs=(spread,) + (P("dp", None),) * 3 + (spread,) * 9,
        out_specs=(spread,) * 9,
        check_vma=False,
    )
```

time: 440 us -> 221 us (0.50)
  Pallas kernels: 0 us -> 188 us
  blocking collectives: 193 us -> 8.59 us
  waiting for transfers between devices: 184 us -> 0 us
  matrix products: 26.3 us -> 0 us
  between operations: 14.2 us -> 0.81 us
    pallas_call x0 -> x1, Pallas kernels: none -> 188 us  [gradient_of(): pl.pallas_call(exchange_kernel, out_shape=jax.ShapeDtypeStruct((rows, wid...]
    all_to_all x1 -> x0, blocking collectives: 186 us -> none  [per_device(): lax.all_to_all(joined, 'dp', split_axis=1, concat_axis=0, tiled=True)]
    all_gather x1 -> x0, waiting for transfers between devices: 184 us -> none  [per_device(): gathered = lax.all_gather(layer_input, 'dp', axis=0, tiled=True)]
    dot_general x1 -> x0, matrix products: 26.3 us -> none  [contract_tokens(): lax.dot_general(cotangent_rows, inputs, (((0,), (0,)), ((), ())), preferr...]
    unnamed x23 -> x19, local copies, waits for them, and re-layouts: 7.01 us -> 8.85 us
  transfers between devices with their start and end apart: 1 -> 0, of which waited for: 1 -> 0; matrix products, arithmetic and copies ran while one was open for 3% -> 0% of each run, Pallas kernels for 0% -> 0%
where the time goes in v1:
time: 221 us
  Pallas kernels  188 us (85%)
  local copies, waits for them, and re-layouts  12.2 us (6%)
  other arithmetic  11.5 us (5%)
  blocking collectives  8.59 us (4%)
    pallas_call x1, Pallas kernels, gradient_of(): pl.pallas_call(exchange_kernel, out_shape=jax.ShapeDtypeStruct((rows, wid...  188 us
    unnamed x19, local copies, waits for them, and re-layouts  8.85 us
    reduce_sum x3, other arithmetic, optimizer_pass(): partial_power = jnp.sum(step * step, axis=1)  8.63 us
    psum x1, blocking collectives, per_device(): lax.psum((power_query, power_key, power_up), 'col')  8.59 us

profile of v1, /device:TPU:1, one launch (start us, length us, event | category | flops | bytes accessed | tf_op | source)
XLA Modules:
  0.0 220.8 jit_solution(17590477025090987629)
XLA Ops:
  0.7 1.1 copy.29
  1.8 1.6 copy.28
  3.5 6.1 %copy.30 = bf16[128,14336]{0,1:T(8,128)(2,1)} copy(bf16[128,14336]{1,0:T(8,128)(2,1)} %param.16) | data formatting | bytes 7340032 | tf_op args[3]
  9.6 1.6 dynamic-slice_bitcast_fusion
  11.2 0.2 maximum_bitcast_fusion
  11.4 1.6 copy.31
  13.1 0.0 copy-start.5
  13.1 0.0 copy-start.6
  13.1 0.0 copy-start.7
  13.1 0.0 copy-start.2
  13.1 0.0 copy-start.3
  13.1 0.0 copy-start.4
  13.1 0.0 copy-start.1
  13.1 187.7 %exchange.1 = f32[304,2048]{1,0:T(8,128)} custom-call(bf16[16,608,128]{2,1,0:T(8,128)(2,1)} %bitcast.12, bf16[128,2048]{1,0:T(8,128)(2,1)} %x_ref.1), custom_call_target="tpu_custom_call" | custom-call | tf_op jit(solution)/shard_map/exchange/pallas_call | solution.py:249
  200.8 0.0 copy-done.5
  200.8 0.0 copy-done.6
  200.8 0.0 copy-done.7
  200.8 0.0 copy-start
  200.9 1.9 multiply_reduce_fusion.2
  202.8 0.0 copy-done.2
  202.8 0.0 copy-done.3
  202.8 0.0 copy-done.4
  202.8 2.3 %multiply_reduce_fusion.1 = (f32[64]{0:T(128)S(1)}, f32[64,2048]{1,0:T(8,128)S(1)}, bf16[64,2048]{1,0:T(8,128)(2,1)}, bf16[64,2048]{1,0:T(8,128)(2,1)}) fusion(bf16[64,2048]{1,0:T(8,128)(2,1)S(1)} %copy-done.2, f32[304,2048]{1,0:T(8,128)} %exchange.1, bf16[64,2048]{1,0:T(8,128)(2,1)S(1)} %copy-done.3, bf16[64,2048]{1,0:T(8,128)(2,1)S(1)} %copy-done.4), kind=kLoop, calls=%fused_computation.13 | loop fusion | flops 2359232 | bytes 2359552 | tf_op jit(solution)/shard_map/reduce_sum | solution.py:274
  205.1 0.0 copy-done.1
  205.2 0.0 copy-done
  205.2 4.4 %multiply_reduce_fusion = (f32[224]{0:T(256)S(1)}, f32[224,2048]{1,0:T(8,128)S(1)}, bf16[224,2048]{1,0:T(8,128)(2,1)}, bf16[224,2048]{1,0:T(8,128)(2,1)}) fusion(bf16[224,2048]{1,0:T(8,128)(2,1)S(1)} %copy-done.1, f32[304,2048]{1,0:T(8,128)S(1)} %copy-done, bf16[224,2048]{1,0:T(8,128)(2,1)} %param.22, bf16[224,2048]{1,0:T(8,128)(2,1)} %param.19), kind=kLoop, calls=%fused_computation.4 | loop fusion | flops 8257312 | bytes 8258432 | tf_op jit(solution)/shard_map/reduce_sum | solution.py:274
  209.5 8.6 %all-reduce = (f32[64]{0:T(128)S(1)}, f32[16]{0:T(128)S(1)}, f32[224]{0:T(256)S(1)}) all-reduce(f32[64]{0:T(128)S(1)} %get-tuple-element.16, f32[16]{0:T(128)S(1)} %get-tuple-element.14, f32[224]{0:T(256)S(1)} %get-tuple-element.12), channel_id=1, replica_groups=mesh['col'=4,'dp'=64] {'col'}, use_global_device_ids=true, to_apply=%region_1.2 | all-reduce | flops 304 | bytes 2432 | tf_op jit(solution)/shard_map/psum | solution.py:330
  218.1 0.8 divide_convert_fusion.1
  219.0 0.7 divide_convert_fusion.2
  219.7 1.1 divide_convert_fusion
  (5 shorter events, 0.1 us)
Async XLA Ops:
  13.1 187.8 %copy-start.5 = (bf16[16,2048]{1,0:T(8,128)(2,1)S(1)}, bf16[16,2048]{1,0:T(8,128)(2,1)}, u32[]{:S(2)}) copy-start(bf16[16,2048]{1,0:T(8,128)(2,1)} %param.24) | copy-start | bytes 196612
  13.1 187.8 %copy-start.6 = (bf16[16,2048]{1,0:T(8,128)(2,1)S(1)}, bf16[16,2048]{1,0:T(8,128)(2,1)}, u32[]{:S(2)}) copy-start(bf16[16,2048]{1,0:T(8,128)(2,1)} %param.21) | copy-start | bytes 196612
  13.1 187.8 %copy-start.7 = (bf16[16,2048]{1,0:T(8,128)(2,1)S(1)}, bf16[16,2048]{1,0:T(8,128)(2,1)}, u32[]{:S(2)}) copy-start(bf16[16,2048]{1,0:T(8,128)(2,1)} %param.18) | copy-start | bytes 196612
  13.1 189.7 %copy-start.2 = (bf16[64,2048]{1,0:T(8,128)(2,1)S(1)}, bf16[64,2048]{1,0:T(8,128)(2,1)}, u32[]{:S(2)}) copy-start(bf16[64,2048]{1,0:T(8,128)(2,1)} %param.23) | copy-start | bytes 786436
  13.1 189.7 %copy-start.3 = (bf16[64,2048]{1,0:T(8,128)(2,1)S(1)}, bf16[64,2048]{1,0:T(8,128)(2,1)}, u32[]{:S(2)}) copy-start(bf16[64,2048]{1,0:T(8,128)(2,1)} %param.20) | copy-start | bytes 786436
  13.1 189.7 %copy-start.4 = (bf16[64,2048]{1,0:T(8,128)(2,1)S(1)}, bf16[64,2048]{1,0:T(8,128)(2,1)}, u32[]{:S(2)}) copy-start(bf16[64,2048]{1,0:T(8,128)(2,1)} %param.17) | copy-start | bytes 786436
  13.1 192.1 %copy-start.1 = (bf16[224,2048]{1,0:T(8,128)(2,1)S(1)}, bf16[224,2048]{1,0:T(8,128)(2,1)}, u32[]{:S(2)}) copy-start(bf16[224,2048]{1,0:T(8,128)(2,1)} %param.25) | copy-start | bytes 2752516
  200.8 4.3 %copy-start = (f32[304,2048]{1,0:T(8,128)S(1)}, f32[304,2048]{1,0:T(8,128)}, u32[]{:S(2)}) copy-start(f32[304,2048]{1,0:T(8,128)} %exchange.1) | copy-start | bytes 7471108

commit v2 on v1

v2 whole, which is shorter than its diff:
```python
import functools

import jax
import jax.numpy as jnp
from jax import lax
from jax.experimental import pallas as pl
from jax.experimental.pallas import tpu as pltpu
from jax.sharding import PartitionSpec as P

beta_one = 0.9
beta_two = 0.95
rate = 0.1
eps_adam = 1e-08
eps_norm = 1e-06

MESH = pl.DeviceIdType.MESH
CHUNKS = 8
LANES = 128


def place():
    dp = lax.axis_index("dp")
    col = lax.axis_index("col")
    return dp // 16, lax.rem(dp // 4, 4), lax.rem(dp, 4), col // 2, lax.rem(col, 2)


def wrap(v):
    return lax.rem(v + 8, 4)


def exchange_kernel(
    x_ref,
    q_ref,
    k_ref,
    u_ref,
    wq_ref,
    wk_ref,
    wu_ref,
    mq_ref,
    mk_ref,
    mu_ref,
    vq_ref,
    vk_ref,
    vu_ref,
    step_ref,
    mean_ref,
    square_ref,
    power_ref,
    stage,
    kt_buf,
    ct_ref,
    opt_buf,
    c_buf,
    x_buf,
    p_buf,
    r_buf,
    lane_power,
    power_in,
    ssem,
    rsem,
    lsem,
):
    y, x, z, lo, core = place()
    rows_of = (wq_ref.shape[0], wk_ref.shape[0], wu_ref.shape[0])
    starts = (0, rows_of[0], rows_of[0] + rows_of[1])
    local = []

    def fetch(src, dst):
        copy = pltpu.make_async_copy(src, dst, lsem.at[len(local)])
        local.append(copy)
        copy.start()
        return copy

    staged = []
    for yy in range(4):
        for ref, n, at in zip((q_ref, k_ref, u_ref), rows_of, starts):
            span = 8 * n
            src = ref.at[:, pl.ds(pl.multiple_of((2 * yy + core) * span, LANES), span)]
            staged.append(fetch(src, stage.at[yy, :, pl.ds(8 * at, span)]))
    toward = 2 * lo - 1
    rows = step_ref.shape[0]
    width = x_ref.shape[1] // CHUNKS

    def device(dy=0, dx=0, dz=0, flip_lo=False, flip_core=False):
        lo_to = 1 - lo if flip_lo else lo
        core_to = 1 - core if flip_core else core
        return {
            "dp": wrap(y + dy) * 16 + wrap(x + dx) * 4 + wrap(z + dz),
            "col": lo_to * 2 + core_to,
        }

    peers = [device(dy=d) for d in (1, 2, 3)]
    peers += [device(dz=d) for d in (1, 2, 3)]
    peers += [device(dx=d) for d in (1, 3)]
    peers += [device(dy=d, dz=toward, flip_lo=True) for d in range(4)]
    peers += [device(dy=d, dz=2, flip_lo=True) for d in range(4)]
    peers += [device(flip_lo=True), device(flip_core=True)]
    peers += [device(flip_lo=True, flip_core=True)]
    barrier = pltpu.get_barrier_semaphore()
    for peer in peers:
        pl.semaphore_signal(barrier, inc=1, device_id=peer, device_id_type=MESH)
    pl.semaphore_wait(barrier, len(peers))

    used = [0]
    pending = []

    def remote(src, dst, to):
        k = used[0]
        used[0] += 1
        return pltpu.make_async_remote_copy(
            src_ref=src,
            dst_ref=dst,
            send_sem=ssem.at[k],
            recv_sem=rsem.at[k],
            device_id=to,
            device_id_type=MESH,
        )

    def go(copy):
        copy.start()
        pending.append(copy)
        return copy

    odd = lax.rem(x, 2)
    inner = (1 - odd, odd)

    def c_block(part, slot):
        return c_buf.at[slot, 2 * core + inner[part]]

    def ct_piece(part, dy, dz):
        return ct_ref.at[wrap(y + dy) * 4 + wrap(z + dz), part]

    def send_c(part, slot, dy, dz, flip):
        to = device(dy=dy, dz=dz, flip_lo=flip)
        return go(remote(ct_piece(part, dy, dz), c_block(part, slot), to))

    def cols(j):
        return pl.ds(j * width, width)

    order = (0, 1, 3, 2)
    side = wrap(-toward)
    mine = wrap(toward)
    facing, far, near, passed, shared = {}, {}, {}, {}, {}

    def c_sends(part):
        facing[part] = [
            send_c(part, wrap(-dy) * 4 + side, dy, toward, True) for dy in order
        ]
        far[part] = [
            send_c(part, wrap(-(lo + 2 * i)) * 4 + 2, lo + 2 * i, 2, True) for i in range(2)
        ]
        near[part] = [send_c(part, ((-dy) % 4) * 4, dy, 0, False) for dy in (1, 3, 2)]

    def z_sends(j):
        return [
            go(
                remote(
                    x_ref.at[:, cols(j)],
                    x_buf.at[pl.ds(((-dz) % 4) * LANES, LANES), cols(j)],
                    device(dz=dz),
                )
            )
            for dz in (1, 3, 2)
        ]

    own_up, own_down, own_fwd = {}, {}, {}

    def halves(h):
        return pl.ds(h * (x_ref.shape[1] // 2), x_ref.shape[1] // 2)

    def own_sends(h):
        at = halves(h)
        src = x_ref.at[:, at]
        own_up[h] = go(remote(src, x_buf.at[pl.ds(12 * LANES, LANES), at], device(dy=1)))
        own_down[h] = go(remote(src, x_buf.at[pl.ds(4 * LANES, LANES), at], device(dy=3)))

    def own_forward(h):
        own_up[h].wait_recv()
        src = x_buf.at[pl.ds(12 * LANES, LANES), halves(h)]
        own_fwd[h] = go(
            remote(src, x_buf.at[pl.ds(8 * LANES, LANES), halves(h)], device(dy=1))
        )

    def own_arrived(h):
        own_down[h].wait_recv()
        own_fwd[h].wait_recv()

    def turn(part):
        xl = inner[part]

        def one(yy, carry):
            if part == 0:
                kt_buf[yy] = stage[yy, :, 8 * starts[1] : 8 * starts[2]].T
            q_span, u_span = 4 * rows_of[0], 4 * rows_of[2]
            q_at = pl.multiple_of(xl * q_span, LANES)
            u_at = pl.multiple_of(8 * starts[2] + xl * u_span, LANES)
            tq = stage[yy, :, pl.ds(q_at, q_span)].T
            tu = stage[yy, :, pl.ds(u_at, u_span)].T
            for zz in range(4):
                to = ct_ref.at[yy * 4 + zz, part]
                n = rows_of[0]
                to[:n] = tq[zz * n : (zz + 1) * n]
                n = rows_of[1]
                k_at = pl.multiple_of(xl * 4 * n + zz * n, 16)
                to[starts[1] : starts[2]] = kt_buf[yy, pl.ds(k_at, n)]
                n = rows_of[2]
                to[starts[2] :] = tu[zz * n : (zz + 1) * n]
            return carry

        lax.fori_loop(0, 4, one, 0)

    own_x = fetch(x_ref, x_buf.at[pl.ds(0, LANES)])
    own_sends(0)
    along_z = {}
    for copy in staged:
        copy.wait()
    turn(0)
    c_sends(0)
    own_c = [fetch(ct_piece(0, 0, 0), c_block(0, 0))]
    turn(1)
    own_c.append(fetch(ct_piece(1, 0, 0), c_block(1, 0)))
    loaded = []
    for i, refs in enumerate(
        ((wq_ref, wk_ref, wu_ref), (mq_ref, mk_ref, mu_ref), (vq_ref, vk_ref, vu_ref))
    ):
        for ref, n, at in zip(refs, rows_of, starts):
            loaded.append(fetch(ref, opt_buf.at[i, pl.ds(at, n)]))

    def share(part, slot):
        at = c_block(part, slot)
        shared[part].append(go(remote(at, at, device(flip_core=True))))

    def pass_on(part, slot):
        at = c_block(part, slot)
        passed[part].append(go(remote(at, at, device(flip_lo=True))))

    def c_direct(part):
        shared[part] = []
        passed[part] = []
        own_c[part].wait()
        share(part, 0)
        for copy, dy in zip(near[part], (1, 3, 2)):
            copy.wait_recv()
            share(part, ((-dy) % 4) * 4)
        if part == 0:
            along_z[0] = z_sends(0)
        for copy, dy in zip(facing[part], order):
            copy.wait_recv()
            slot = wrap(-dy) * 4 + mine
            pass_on(part, slot)
            share(part, slot)
        for i, copy in enumerate(far[part]):
            copy.wait_recv()
            slot = wrap(-((1 - lo) + 2 * i)) * 4 + 2
            pass_on(part, slot)
            share(part, slot)

    def c_passed(part):
        for copy, dy in zip(passed[part][:4], order):
            copy.wait_recv()
            share(part, wrap(-dy) * 4 + side)
        for i, copy in enumerate(passed[part][4:]):
            copy.wait_recv()
            share(part, wrap(-(lo + 2 * i)) * 4 + 2)

    def c_ready(part):
        for copy in shared[part]:
            copy.wait_recv()

    up, down, fwd_up, fwd_down = {}, {}, {}, {}

    def stage_y(j):
        for copy in along_z[j]:
            copy.wait_recv()
        if j + 2 < CHUNKS:
            along_z[j + 2] = z_sends(j + 2)
        src = x_buf.at[pl.ds(LANES, 3 * LANES), cols(j)]
        up[j] = go(remote(src, x_buf.at[pl.ds(13 * LANES, 3 * LANES), cols(j)], device(dy=1)))
        down[j] = go(remote(src, x_buf.at[pl.ds(5 * LANES, 3 * LANES), cols(j)], device(dy=3)))

    def stage_forward(j):
        up[j].wait_recv()
        fwd_up[j] = go(
            remote(
                x_buf.at[pl.ds(13 * LANES, LANES), cols(j)],
                x_buf.at[pl.ds(9 * LANES, LANES), cols(j)],
                device(dy=1),
            )
        )
        down[j].wait_recv()
        fwd_down[j] = go(
            remote(
                x_buf.at[pl.ds(6 * LANES, 2 * LANES), cols(j)],
                x_buf.at[pl.ds(10 * LANES, 2 * LANES), cols(j)],
                device(dy=3),
            )
        )

    ring = {}

    def ring_send(j, step):
        for way, sign in ((0, 1), (1, -1)):
            target = wrap(x - sign * (step + 1))
            if step > 0:
                ring[j, step - 1, way].wait_recv()
                p_buf[j, target, way] = p_buf[j, target, way] + r_buf[j, step - 1, way]
            ring[j, step, way] = go(
                remote(p_buf.at[j, target, way], r_buf.at[j, step, way], device(dx=sign))
            )

    def finish(j):
        if j == 0:
            for copy in loaded:
                copy.wait()
            lane_power[...] = jnp.zeros_like(lane_power)
        for way in (0, 1):
            ring[j, 2, way].wait_recv()
            at = pl.ds(j * width + way * (width // 2), width // 2)
            gradient = p_buf[j, x, way] + r_buf[j, 2, way]
            weight = opt_buf[0, :, at].astype(jnp.float32)
            moment = opt_buf[1, :, at].astype(jnp.float32)
            second = opt_buf[2, :, at].astype(jnp.float32)
            first = beta_one * moment + (1.0 - beta_one) * gradient
            square = beta_two * second + (1.0 - beta_two) * gradient * gradient
            step = weight - rate * first / (jnp.sqrt(square) + eps_adam)
            mean_ref[:, at] = first.astype(jnp.bfloat16)
            square_ref[:, at] = square.astype(jnp.bfloat16)
            step_ref[:, at] = step
            lane_power[...] += step * step

    def gather_power():
        ones = jnp.ones((8, LANES), jnp.float32)
        power_in[0] = lax.dot_general(
            ones,
            lane_power[...],
            (((1,), (1,)), ((), ())),
            precision=lax.Precision.HIGHEST,
            preferred_element_type=jnp.float32,
        )
        copies = [
            go(remote(power_in.at[0], power_in.at[i], to))
            for i, to in (
                (1, device(flip_core=True)),
                (2, device(flip_lo=True)),
                (3, device(flip_lo=True, flip_core=True)),
            )
        ]
        for copy in copies:
            copy.wait_recv()
        pair = [power_in[0] + power_in[1], power_in[2] + power_in[3]]
        power_ref[...] = pair[0] + pair[1]

    def multiply(j, part):
        def one(i, carry):
            d = wrap(x + 1 + part + 2 * i)
            lhs = jnp.concatenate([c_buf[k, d] for k in range(16)], axis=1)
            out = jnp.dot(lhs, x_buf[:, cols(j)], preferred_element_type=jnp.float32)
            p_buf[j, d, 0] = out[:, : width // 2]
            p_buf[j, d, 1] = out[:, width // 2 :]
            return carry

        lax.fori_loop(0, 2, one, 0)

    def arrived(j):
        fwd_up[j].wait_recv()
        fwd_down[j].wait_recv()

    c_direct(0)
    c_sends(1)
    along_z[1] = z_sends(1)
    own_forward(0)
    stage_y(0)
    c_passed(0)
    c_ready(0)
    stage_forward(0)
    own_sends(1)
    stage_y(1)
    c_direct(1)
    own_x.wait()
    own_arrived(0)
    arrived(0)
    multiply(0, 0)
    ring_send(0, 0)
    stage_forward(1)
    c_passed(1)
    stage_y(2)
    own_forward(1)
    c_ready(1)
    multiply(0, 1)

    for j in range(1, CHUNKS + 4):
        if j == CHUNKS // 2:
            own_arrived(1)
        if j < CHUNKS:
            arrived(j)
            multiply(j, 0)
            ring_send(j, 0)
        if j + 1 < CHUNKS:
            stage_forward(j + 1)
        if j < CHUNKS:
            multiply(j, 1)
        if 0 <= j - 1 < CHUNKS:
            ring_send(j - 1, 1)
        if j + 2 < CHUNKS:
            stage_y(j + 2)
        if 0 <= j - 2 < CHUNKS:
            ring_send(j - 2, 2)
        if 0 <= j - 4 < CHUNKS:
            finish(j - 4)
    gather_power()
    for copy in pending:
        copy.wait_send()


def final_kernel(
    step_ref,
    mean_ref,
    square_ref,
    power_ref,
    new_q,
    new_k,
    new_u,
    mean_q,
    mean_k,
    mean_u,
    square_q,
    square_k,
    square_u,
):
    total = power_ref[...].T[:, :1]
    width = 4 * step_ref.shape[1]
    scale = 1.0 / jnp.sqrt(total / width + eps_norm)
    at = 0
    for new, mean, square in (
        (new_q, mean_q, square_q),
        (new_k, mean_k, square_k),
        (new_u, mean_u, square_u),
    ):
        rows = pl.ds(at, new.shape[0])
        part = scale[at : at + new.shape[0]]
        new[...] = (step_ref[rows, :] * part).astype(jnp.bfloat16)
        mean[...] = mean_ref[rows, :]
        square[...] = square_ref[rows, :]
        at += new.shape[0]


def per_device(*arguments):
    layer_input = arguments[0]
    weights = arguments[4:7]
    tokens, width = layer_input.shape
    rows = sum(w.shape[0] for w in weights)
    chunk = width // CHUNKS
    count = 2 * (9 + 6 + 16) + 6 + CHUNKS * (3 + 4 + 6) + 3
    vmem = pl.BlockSpec(memory_space=pltpu.VMEM)
    step, mean, square, power = pl.pallas_call(
        exchange_kernel,
        out_shape=(
            jax.ShapeDtypeStruct((rows, width), jnp.float32),
            jax.ShapeDtypeStruct((rows, width), jnp.bfloat16),
            jax.ShapeDtypeStruct((rows, width), jnp.bfloat16),
            jax.ShapeDtypeStruct((8, rows), jnp.float32),
        ),
        in_specs=[pl.BlockSpec(memory_space=pl.ANY)] * 13,
        out_specs=(vmem,) * 4,
        scratch_shapes=[
            pltpu.VMEM((4, tokens, 8 * rows), jnp.bfloat16),
            pltpu.VMEM((4, LANES, tokens), jnp.bfloat16),
            pltpu.VMEM((16, 2, rows, tokens), jnp.bfloat16),
            pltpu.VMEM((3, rows, width), jnp.bfloat16),
            pltpu.VMEM((16, 4, rows, tokens), jnp.bfloat16),
            pltpu.VMEM((16 * tokens, width), jnp.bfloat16),
            pltpu.VMEM((CHUNKS, 4, 2, rows, chunk // 2), jnp.float32),
            pltpu.VMEM((CHUNKS, 3, 2, rows, chunk // 2), jnp.float32),
            pltpu.VMEM((rows, LANES), jnp.float32),
            pltpu.VMEM((4, 8, rows), jnp.float32),
            pltpu.SemaphoreType.DMA((count,)),
            pltpu.SemaphoreType.DMA((count,)),
            pltpu.SemaphoreType.DMA((12 + 1 + 2 + 9,)),
        ],
        compiler_params=pltpu.CompilerParams(
            collective_id=0, has_side_effects=True, vmem_limit_bytes=60 << 20
        ),
        name="exchange",
    )(*arguments)
    shapes = tuple(jax.ShapeDtypeStruct(w.shape, jnp.bfloat16) for w in weights)
    return pl.pallas_call(
        final_kernel,
        out_shape=shapes * 3,
        in_specs=[vmem] * 4,
        out_specs=(vmem,) * 9,
        compiler_params=pltpu.CompilerParams(vmem_limit_bytes=40 << 20),
        name="final",
    )(step, mean, square, power)


def solution(mesh):
    spread = P("dp", "col")
    return jax.shard_map(
        per_device,
        mesh=mesh,
        in_specs=(spread,) + (P("dp", None),) * 3 + (spread,) * 9,
        out_specs=(spread,) * 9,
        check_vma=False,
    )
```

time: 221 us -> 178 us (0.81)
  Pallas kernels: 188 us -> 173 us
  other arithmetic: 11.5 us -> 0 us
  blocking collectives: 8.59 us -> 0 us
  local copies, waits for them, and re-layouts: 12.2 us -> 4.99 us
    pallas_call x1 -> x2, Pallas kernels: 188 us -> 173 us  [the longest x1 170 us: per_device(): pl.pallas_call(exchange_kernel, out_shape=(jax.ShapeDtypeStruct((rows, wi...]
    reduce_sum x3 -> x0, other arithmetic: 8.63 us -> none  [optimizer_pass(): partial_power = jnp.sum(step * step, axis=1)]
    psum x1 -> x0, blocking collectives: 8.59 us -> none  [per_device(): lax.psum((power_query, power_key, power_up), 'col')]
    unnamed x19 -> x8, local copies, waits for them, and re-layouts: 8.85 us -> 4.99 us
    convert_element_type x3 -> x0, other arithmetic: 2.68 us -> none  [finish_rows(): return (step / scale[:, None]).astype(jnp.bfloat16)]
where the time goes in v2:
time: 178 us
  Pallas kernels  173 us (97%)
  local copies, waits for them, and re-layouts  4.99 us (3%)
    pallas_call x1, Pallas kernels, per_device(): pl.pallas_call(exchange_kernel, out_shape=(jax.ShapeDtypeStruct((rows, wi...  170 us
    unnamed x8, local copies, waits for them, and re-layouts  4.99 us

profile of v2, /device:TPU:1, one launch (start us, length us, event | category | flops | bytes accessed | tf_op | source)
XLA Modules:
  0.0 178.2 jit_solution(2840542518803353040)
XLA Ops:
  0.6 170.4 %exchange.1 = (f32[304,2048]{1,0:T(8,128)}, bf16[304,2048]{1,0:T(8,128)(2,1)}, bf16[304,2048]{1,0:T(8,128)(2,1)}, f32[8,304]{1,0:T(8,128)}) custom-call(bf16[128,2048]{1,0:T(8,128)(2,1)} %x_ref.1, bf16[128,4096]{1,0:T(8,128)(2,1)} %q_ref.1, bf16[128,1024]{1,0:T(8,128)(2,1)} %k_ref.1, bf16[128,14336]{1,0:T(8,128)(2,1)} %u_ref.1, bf16[64,2048]{1,0:T(8,128)(2,1)} %wq_ref.1, ...), custom_call_target="tpu_custom_call" | custom-call | tf_op jit(solution)/shard_map/exchange/pallas_call | solution.py:455
  171.0 0.0 copy-start
  171.0 1.7 copy-done
  172.7 0.0 copy-start.1
  172.7 1.3 copy-done.1
  174.0 0.0 copy-start.2
  174.0 1.3 copy-done.2
  175.3 0.0 copy-start.3
  175.3 0.7 copy-done.3
  176.0 2.1 %final.1 = (bf16[64,2048]{1,0:T(8,128)(2,1)}, bf16[16,2048]{1,0:T(8,128)(2,1)}, bf16[224,2048]{1,0:T(8,128)(2,1)}, bf16[64,2048]{1,0:T(8,128)(2,1)}, bf16[16,204...) custom-call(f32[304,2048]{1,0:T(8,128)S(1)} %copy-done, ...), custom_call_target="tpu_custom_call" | custom-call | tf_op jit(solution)/shard_map/final/pallas_call | solution.py:486
Async XLA Ops:
  171.0 1.7 copy-start
  172.7 1.3 copy-start.1
  174.0 1.3 copy-start.2
  175.3 0.7 copy-start.3

commit v3 on v2

--- a/solution.py
+++ b/solution.py
@@ -14,8 +14,10 @@
 eps_norm = 1e-06
 
 MESH = pl.DeviceIdType.MESH
-CHUNKS = 8
 LANES = 128
+WIDTHS = (256,) * 8
+STARTS = tuple(sum(WIDTHS[:j]) for j in range(len(WIDTHS)))
+CHUNKS = len(WIDTHS)
 
 
 def place():
@@ -79,7 +81,6 @@
             staged.append(fetch(src, stage.at[yy, :, pl.ds(8 * at, span)]))
     toward = 2 * lo - 1
     rows = step_ref.shape[0]
-    width = x_ref.shape[1] // CHUNKS
 
     def device(dy=0, dx=0, dz=0, flip_lo=False, flip_core=False):
         lo_to = 1 - lo if flip_lo else lo
@@ -135,7 +136,7 @@
         return go(remote(ct_piece(part, dy, dz), c_block(part, slot), to))
 
     def cols(j):
-        return pl.ds(j * width, width)
+        return pl.ds(STARTS[j], WIDTHS[j])
 
     order = (0, 1, 3, 2)
     side = wrap(-toward)
@@ -209,71 +210,11 @@
 
         lax.fori_loop(0, 4, one, 0)
 
-    own_x = fetch(x_ref, x_buf.at[pl.ds(0, LANES)])
-    own_sends(0)
-    along_z = {}
-    for copy in staged:
-        copy.wait()
-    turn(0)
-    c_sends(0)
-    own_c = [fetch(ct_piece(0, 0, 0), c_block(0, 0))]
-    turn(1)
-    own_c.append(fetch(ct_piece(1, 0, 0), c_block(1, 0)))
-    loaded = []
-    for i, refs in enumerate(
-        ((wq_ref, wk_ref, wu_ref), (mq_ref, mk_ref, mu_ref), (vq_ref, vk_ref, vu_ref))
-    ):
-        for ref, n, at in zip(refs, rows_of, starts):
-            loaded.append(fetch(ref, opt_buf.at[i, pl.ds(at, n)]))
-
-    def share(part, slot):
-        at = c_block(part, slot)
-        shared[part].append(go(remote(at, at, device(flip_core=True))))
-
-    def pass_on(part, slot):
-        at = c_block(part, slot)
-        passed[part].append(go(remote(at, at, device(flip_lo=True))))
-
-    def c_direct(part):
-        shared[part] = []
-        passed[part] = []
-        own_c[part].wait()
-        share(part, 0)
-        for copy, dy in zip(near[part], (1, 3, 2)):
-            copy.wait_recv()
-            share(part, ((-dy) % 4) * 4)
-        if part == 0:
-            along_z[0] = z_sends(0)
-        for copy, dy in zip(facing[part], order):
-            copy.wait_recv()
-            slot = wrap(-dy) * 4 + mine
-            pass_on(part, slot)
-            share(part, slot)
-        for i, copy in enumerate(far[part]):
-            copy.wait_recv()
-            slot = wrap(-((1 - lo) + 2 * i)) * 4 + 2
-            pass_on(part, slot)
-            share(part, slot)
-
-    def c_passed(part):
-        for copy, dy in zip(passed[part][:4], order):
-            copy.wait_recv()
-            share(part, wrap(-dy) * 4 + side)
-        for i, copy in enumerate(passed[part][4:]):
-            copy.wait_recv()
-            share(part, wrap(-(lo + 2 * i)) * 4 + 2)
-
-    def c_ready(part):
-        for copy in shared[part]:
-            copy.wait_recv()
-
     up, down, fwd_up, fwd_down = {}, {}, {}, {}
 
     def stage_y(j):
         for copy in along_z[j]:
             copy.wait_recv()
-        if j + 2 < CHUNKS:
-            along_z[j + 2] = z_sends(j + 2)
         src = x_buf.at[pl.ds(LANES, 3 * LANES), cols(j)]
         up[j] = go(remote(src, x_buf.at[pl.ds(13 * LANES, 3 * LANES), cols(j)], device(dy=1)))
         down[j] = go(remote(src, x_buf.at[pl.ds(5 * LANES, 3 * LANES), cols(j)], device(dy=3)))
@@ -296,16 +237,85 @@
             )
         )
 
+    own_x = fetch(x_ref, x_buf.at[pl.ds(0, LANES)])
+    own_sends(0)
+    along_z = {0: z_sends(0)}
+    for copy in staged:
+        copy.wait()
+    turn(0)
+    c_sends(0)
+    own_c = [fetch(ct_piece(0, 0, 0), c_block(0, 0))]
+    stage_y(0)
+    own_forward(0)
+    own_sends(1)
+    turn(1)
+    own_c.append(fetch(ct_piece(1, 0, 0), c_block(1, 0)))
+    loaded = []
+    for i, refs in enumerate(
+        ((wq_ref, wk_ref, wu_ref), (mq_ref, mk_ref, mu_ref), (vq_ref, vk_ref, vu_ref))
+    ):
+        for ref, n, at in zip(refs, rows_of, starts):
+            loaded.append(fetch(ref, opt_buf.at[i, pl.ds(at, n)]))
+
+    def share(part, slot):
+        at = c_block(part, slot)
+        shared[part].append(go(remote(at, at, device(flip_core=True))))
+
+    def pass_on(part, slot):
+        at = c_block(part, slot)
+        passed[part].append(go(remote(at, at, device(flip_lo=True))))
+
+    def c_direct(part, after_near, after_facing, after_far):
+        shared[part] = []
+        passed[part] = []
+        own_c[part].wait()
+        share(part, 0)
+        for copy, dy in zip(near[part], (1, 3, 2)):
+            copy.wait_recv()
+            share(part, ((-dy) % 4) * 4)
+        after_near()
+        for copy, dy in zip(facing[part], order):
+            copy.wait_recv()
+            slot = wrap(-dy) * 4 + mine
+            pass_on(part, slot)
+            share(part, slot)
+        after_facing()
+        for i, copy in enumerate(far[part]):
+            copy.wait_recv()
+            slot = wrap(-((1 - lo) + 2 * i)) * 4 + 2
+            pass_on(part, slot)
+            share(part, slot)
+        after_far()
+
+    def z_issue(j):
+        along_z[j] = z_sends(j)
+
+    def c_passed(part):
+        for copy, dy in zip(passed[part][:4], order):
+            copy.wait_recv()
+            share(part, wrap(-dy) * 4 + side)
+        for i, copy in enumerate(passed[part][4:]):
+            copy.wait_recv()
+            share(part, wrap(-(lo + 2 * i)) * 4 + 2)
+
+    def c_ready(part):
+        for copy in shared[part]:
+            copy.wait_recv()
+
     ring = {}
+
+    def rows_way(way):
+        return pl.ds(way * (rows // 2), rows // 2)
 
     def ring_send(j, step):
         for way, sign in ((0, 1), (1, -1)):
             target = wrap(x - sign * (step + 1))
+            at = (rows_way(way), cols(j))
             if step > 0:
                 ring[j, step - 1, way].wait_recv()
-                p_buf[j, target, way] = p_buf[j, target, way] + r_buf[j, step - 1, way]
+                p_buf[(target,) + at] = p_buf[(target,) + at] + r_buf[(step - 1,) + at]
             ring[j, step, way] = go(
-                remote(p_buf.at[j, target, way], r_buf.at[j, step, way], device(dx=sign))
+                remote(p_buf.at[(target,) + at], r_buf.at[(step,) + at], device(dx=sign))
             )
 
     def finish(j):
@@ -315,8 +325,9 @@
             lane_power[...] = jnp.zeros_like(lane_power)
         for way in (0, 1):
             ring[j, 2, way].wait_recv()
-            at = pl.ds(j * width + way * (width // 2), width // 2)
-            gradient = p_buf[j, x, way] + r_buf[j, 2, way]
+        for lane in range(STARTS[j], STARTS[j] + WIDTHS[j], LANES):
+            at = pl.ds(lane, LANES)
+            gradient = p_buf[x, :, at] + r_buf[2, :, at]
             weight = opt_buf[0, :, at].astype(jnp.float32)
             moment = opt_buf[1, :, at].astype(jnp.float32)
             second = opt_buf[2, :, at].astype(jnp.float32)
@@ -355,8 +366,7 @@
             d = wrap(x + 1 + part + 2 * i)
             lhs = jnp.concatenate([c_buf[k, d] for k in range(16)], axis=1)
             out = jnp.dot(lhs, x_buf[:, cols(j)], preferred_element_type=jnp.float32)
-            p_buf[j, d, 0] = out[:, : width // 2]
-            p_buf[j, d, 1] = out[:, width // 2 :]
+            p_buf[d, :, cols(j)] = out
             return carry
 
         lax.fori_loop(0, 2, one, 0)
@@ -365,44 +375,57 @@
         fwd_up[j].wait_recv()
         fwd_down[j].wait_recv()
 
-    c_direct(0)
-    c_sends(1)
-    along_z[1] = z_sends(1)
-    own_forward(0)
-    stage_y(0)
+    def early():
+        z_issue(1)
+        stage_forward(0)
+
+    c_direct(0, early, lambda: None, lambda: c_sends(1))
+    stage_y(1)
     c_passed(0)
+    own_forward(1)
     c_ready(0)
-    stage_forward(0)
-    own_sends(1)
-    stage_y(1)
-    c_direct(1)
     own_x.wait()
     own_arrived(0)
     arrived(0)
     multiply(0, 0)
     ring_send(0, 0)
-    stage_forward(1)
+    c_direct(1, lambda: z_issue(2), lambda: stage_forward(1), lambda: z_issue(3))
+    stage_y(2)
+    arrived(1)
+    multiply(1, 0)
+    ring_send(1, 0)
     c_passed(1)
-    stage_y(2)
-    own_forward(1)
+    z_issue(4)
     c_ready(1)
     multiply(0, 1)
-
-    for j in range(1, CHUNKS + 4):
-        if j == CHUNKS // 2:
+    ring_send(0, 1)
+    stage_y(3)
+    z_issue(5)
+    stage_forward(2)
+    multiply(1, 1)
+    ring_send(1, 1)
+
+    ys, zs = 4, 6
+    half_at = min(j for j in range(CHUNKS) if STARTS[j] + WIDTHS[j] > x_ref.shape[1] // 2)
+    for j in range(2, CHUNKS + 4):
+        if j == half_at:
             own_arrived(1)
         if j < CHUNKS:
             arrived(j)
             multiply(j, 0)
             ring_send(j, 0)
+        while ys < min(j + 3, CHUNKS):
+            stage_y(ys)
+            ys += 1
+            if zs < CHUNKS:
+                z_issue(zs)
+                zs += 1
         if j + 1 < CHUNKS:
             stage_forward(j + 1)
         if j < CHUNKS:
             multiply(j, 1)
-        if 0 <= j - 1 < CHUNKS:
+        if 2 <= j - 1 < CHUNKS:
             ring_send(j - 1, 1)
-        if j + 2 < CHUNKS:
-            stage_y(j + 2)
         if 0 <= j - 2 < CHUNKS:
             ring_send(j - 2, 2)
         if 0 <= j - 4 < CHUNKS:
@@ -412,36 +435,42 @@
         copy.wait_send()
 
 
-def final_kernel(
-    step_ref,
-    mean_ref,
-    square_ref,
-    power_ref,
-    new_q,
-    new_k,
-    new_u,
-    mean_q,
-    mean_k,
-    mean_u,
-    square_q,
-    square_k,
-    square_u,
-):
-    total = power_ref[...].T[:, :1]
-    width = 4 * step_ref.shape[1]
-    scale = 1.0 / jnp.sqrt(total / width + eps_norm)
-    at = 0
-    for new, mean, square in (
-        (new_q, mean_q, square_q),
-        (new_k, mean_k, square_k),
-        (new_u, mean_u, square_u),
-    ):
-        rows = pl.ds(at, new.shape[0])
-        part = scale[at : at + new.shape[0]]
-        new[...] = (step_ref[rows, :] * part).astype(jnp.bfloat16)
-        mean[...] = mean_ref[rows, :]
-        square[...] = square_ref[rows, :]
-        at += new.shape[0]
+def final_kernel(*refs):
+    step_ref, mean_ref, square_ref, power_ref = refs[:4]
+    outputs = refs[4:13]
+    step_buf, mean_buf, square_buf, power_buf, new_buf, sems = refs[13:]
+    started = []
+
+    def move(src, dst):
+        copy = pltpu.make_async_copy(src, dst, sems.at[len(started)])
+        started.append(copy)
+        copy.start()
+        return copy
+
+    def spread(buf, targets):
+        at = 0
+        for target in targets:
+            rows = target.shape[0]
+            leaving.append(move(buf.at[pl.ds(at, rows)], target))
+            at += rows
+
+    leaving = []
+    power = move(power_ref, power_buf)
+    step = move(step_ref, step_buf)
+    mean = move(mean_ref, mean_buf)
+    square = move(square_ref, square_buf)
+    power.wait()
+    total = power_buf[...].T[:, :1]
+    scale = 1.0 / jnp.sqrt(total / (4 * step_buf.shape[1]) + eps_norm)
+    step.wait()
+    new_buf[...] = (step_buf[...] * scale).astype(jnp.bfloat16)
+    mean.wait()
+    spread(mean_buf, outputs[3:6])
+    square.wait()
+    spread(square_buf, outputs[6:9])
+    spread(new_buf, outputs[0:3])
+    for copy in leaving:
+        copy.wait()
 
 
 def per_device(*arguments):
@@ -449,9 +478,9 @@
     weights = arguments[4:7]
     tokens, width = layer_input.shape
     rows = sum(w.shape[0] for w in weights)
-    chunk = width // CHUNKS
     count = 2 * (9 + 6 + 16) + 6 + CHUNKS * (3 + 4 + 6) + 3
     vmem = pl.BlockSpec(memory_space=pltpu.VMEM)
+    hbm = pl.BlockSpec(memory_space=pl.ANY)
     step, mean, square, power = pl.pallas_call(
         exchange_kernel,
         out_shape=(
@@ -469,8 +498,8 @@
             pltpu.VMEM((3, rows, width), jnp.bfloat16),
             pltpu.VMEM((16, 4, rows, tokens), jnp.bfloat16),
             pltpu.VMEM((16 * tokens, width), jnp.bfloat16),
-            pltpu.VMEM((CHUNKS, 4, 2, rows, chunk // 2), jnp.float32),
-            pltpu.VMEM((CHUNKS, 3, 2, rows, chunk // 2), jnp.float32),
+            pltpu.VMEM((4, rows, width), jnp.float32),
+            pltpu.VMEM((3, rows, width), jnp.float32),
             pltpu.VMEM((rows, LANES), jnp.float32),
             pltpu.VMEM((4, 8, rows), jnp.float32),
             pltpu.SemaphoreType.DMA((count,)),
@@ -486,9 +515,17 @@
     return pl.pallas_call(
         final_kernel,
         out_shape=shapes * 3,
-        in_specs=[vmem] * 4,
-        out_specs=(vmem,) * 9,
-        compiler_params=pltpu.CompilerParams(vmem_limit_bytes=40 << 20),
+        in_specs=[hbm] * 4,
+        out_specs=(hbm,) * 9,
+        scratch_shapes=[
+            pltpu.VMEM((rows, width), jnp.float32),
+            pltpu.VMEM((rows, width), jnp.bfloat16),
+            pltpu.VMEM((rows, width), jnp.bfloat16),
+            pltpu.VMEM((8, rows), jnp.float32),
+            pltpu.VMEM((rows, width), jnp.bfloat16),
+            pltpu.SemaphoreType.DMA((13,)),
+        ],
+        compiler_params=pltpu.CompilerParams(vmem_limit_bytes=60 << 20),
         name="final",
     )(step, mean, square, power)
 

time: 178 us -> 171 us (0.961)
  local copies, waits for them, and re-layouts: 4.99 us -> 0 us
  Pallas kernels: 173 us -> 170 us
    unnamed x8 -> x0, local copies, waits for them, and re-layouts: 4.99 us -> none
    pallas_call x1, Pallas kernels: 170 us -> 166 us  [per_device(): pl.pallas_call(exchange_kernel, out_shape=(jax.ShapeDtypeStruct((rows, wi...]
    pallas_call x1, Pallas kernels: 2.12 us -> 4.02 us  [per_device(): pl.pallas_call(final_kernel, out_shape=shapes * 3, in_specs=[hbm] * 4, ou...]
where the time goes in v3:
time: 171 us
  Pallas kernels  170 us (99%)
    pallas_call x1, Pallas kernels, per_device(): pl.pallas_call(exchange_kernel, out_shape=(jax.ShapeDtypeStruct((rows, wi...  166 us
    pallas_call x1, Pallas kernels, per_device(): pl.pallas_call(final_kernel, out_shape=shapes * 3, in_specs=[hbm] * 4, ou...  4.02 us

profile of v3, /device:TPU:1, one launch (start us, length us, event | category | flops | bytes accessed | tf_op | source)
XLA Modules:
  0.0 171.0 jit_solution(1753682965846016470)
XLA Ops:
  0.6 166.1 %exchange.1 = (f32[304,2048]{1,0:T(8,128)}, bf16[304,2048]{1,0:T(8,128)(2,1)}, bf16[304,2048]{1,0:T(8,128)(2,1)}, f32[8,304]{1,0:T(8,128)}) custom-call(bf16[128,2048]{1,0:T(8,128)(2,1)} %x_ref.1, bf16[128,4096]{1,0:T(8,128)(2,1)} %q_ref.1, bf16[128,1024]{1,0:T(8,128)(2,1)} %k_ref.1, bf16[128,14336]{1,0:T(8,128)(2,1)} %u_ref.1, bf16[64,2048]{1,0:T(8,128)(2,1)} %wq_ref.1, ...), custom_call_target="tpu_custom_call" | custom-call | tf_op jit(solution)/shard_map/exchange/pallas_call | solution.py:484
  166.8 4.0 %final.1 = (bf16[64,2048]{1,0:T(8,128)(2,1)}, bf16[16,2048]{1,0:T(8,128)(2,1)}, bf16[224,2048]{1,0:T(8,128)(2,1)}, bf16[64,2048]{1,0:T(8,128)(2,1)}, bf16[16,204...) custom-call(f32[304,2048]{1,0:T(8,128)} %get-tuple-element.13.refs_0, ...), custom_call_target="tpu_custom_call" | custom-call | tf_op jit(solution)/shard_map/final/pallas_call | solution.py:515
